TPU v7x, 32 devices: a whole 2x2x4 slice. The times are simulated.
32 devices in a mesh: gx: 4 (over z), gy: 8 (over y, x, core).
Axes of the slice: x: 2, y: 2, z: 4, core: 2. Of those that a mesh axis runs over, the one named last changes fastest.
Arguments:
- particles: bfloat16 [2048, 4096], P(('gx', 'gy')), may hold values from -6 to 6
- references: bfloat16 [4, 12, 4096], P('gx'), may hold values from -1 to 1
- slot_class: int32 [4], replicated, may hold values from 0 to 3, each once
- log_prior: float32 [4], replicated, may hold values from -2 to 2
- shift_offsets: int32 [8, 2], replicated, may hold values from -8 to 8
- group_ids: int32 [2048], P(('gx', 'gy')), may hold values from 0 to 127
- ctf_table: float32 [128, 2048], replicated, may hold values from -1 to 1
- noise_power: float32 [2048], replicated, may hold values from 0.5 to 2
Outputs:
- class_sums: float32 [4, 12, 4096], P('gx')
- ctf_power: float32 [4, 2048], P('gx')
- log_evidence: float32 [], replicated
Inputs may be any that keep to these rules, and one draw needn't show every extreme that they name: `slot_class`: each class id stands at exactly one slot.
All inputs are finite; a program needn't handle non-finite values.
Results may differ from a plain program's by a relative error of at most 0.006.
Values may be sent and summed in bfloat16 or wider, within the bound.
No kernel may reach another device: no remote copies, remote signals or barrier semaphores. Data moves between devices by JAX's collectives and lax.ppermute only.
A program may use at most 64 MiB of HBM per device.

v0:
```python
import jax
import jax.numpy as jnp
from jax import lax
from jax.sharding import PartitionSpec as P

L = 64
R = 12
NS = 8
G = 128
HALF = 2048
FR = 4096


def phase_tables(shift_offsets, edge_len):
    half_size = edge_len * edge_len // 2
    freq_index = jnp.arange(half_size, dtype=jnp.int32)
    row_freq = freq_index // (edge_len // 2)
    col_freq = freq_index % (edge_len // 2)
    phase_turns = jnp.mod(
        row_freq[None, :] * shift_offsets[:, 0:1] + col_freq[None, :] * shift_offsets[:, 1:2],
        edge_len,
    )
    angles = phase_turns.astype(jnp.float32) * (2.0 * jnp.pi / edge_len)
    return (jnp.cos(angles), jnp.sin(angles))


def spectra(particles, edge_len):
    rows_here = particles.shape[0]
    half_side = edge_len // 2
    images = particles.astype(jnp.float32).reshape(rows_here * edge_len, edge_len)
    pixel_index = jnp.arange(edge_len, dtype=jnp.int32)
    column_turns = jnp.mod(pixel_index[:, None] * pixel_index[None, :half_side], edge_len).astype(
        jnp.float32
    ) * (2.0 * jnp.pi / edge_len)
    column_table = jnp.concatenate([jnp.cos(column_turns), -jnp.sin(column_turns)], axis=1)
    partial_x = jnp.dot(
        images, column_table, precision=lax.Precision.HIGHEST, preferred_element_type=jnp.float32
    )
    partial_x = partial_x.reshape(rows_here, edge_len, edge_len)
    row_turns = jnp.mod(pixel_index[:, None] * pixel_index[None, :], edge_len).astype(
        jnp.float32
    ) * (2.0 * jnp.pi / edge_len)
    with_cos = jnp.einsum(
        "uy,pyw->puw", jnp.cos(row_turns), partial_x, precision=lax.Precision.HIGHEST
    )
    with_sin = jnp.einsum(
        "uy,pyw->puw", jnp.sin(row_turns), partial_x, precision=lax.Precision.HIGHEST
    )
    real_part = (with_cos[..., :half_side] + with_sin[..., half_side:]) / edge_len
    imag_part = (with_cos[..., half_side:] - with_sin[..., :half_side]) / edge_len
    return (real_part.reshape(rows_here, -1), imag_part.reshape(rows_here, -1))


def shards(
    particles, references, slot_class, log_prior, shift_offsets, group_ids, ctf_table, noise_power
):
    rows_here = particles.shape[0]
    classes = lax.axis_size("gx") * references.shape[0]
    row_width = R * NS
    real_part, imag_part = spectra(particles, L)
    inv_noise = 1.0 / noise_power
    group_hot = (group_ids[:, None] == jnp.arange(G, dtype=jnp.int32)[None, :]).astype(jnp.float32)
    ctf_rows = jnp.dot(
        group_hot, ctf_table, precision=lax.Precision.HIGHEST, preferred_element_type=jnp.float32
    )
    whiten = ctf_rows * inv_noise
    weighted = jnp.concatenate([real_part * whiten, imag_part * whiten], axis=1).astype(
        jnp.bfloat16
    )
    data_power = jnp.sum((real_part * real_part + imag_part * imag_part) * inv_noise, axis=1)
    cosines, sine_table = phase_tables(shift_offsets, L)
    power_table = ctf_table * ctf_table * inv_noise
    blank = jnp.zeros((rows_here, classes * row_width), jnp.float32)
    piece = lax.all_gather(references, "gx", axis=0, tiled=True)

    def add_class(offset, table):
        stack_row = lax.dynamic_index_in_dim(piece, offset, 0, keepdims=False).astype(jnp.float32)
        stack_real = stack_row[:, :HALF]
        stack_imag = stack_row[:, HALF:]
        shifted_real = (
            stack_real[:, None, :] * cosines[None] + stack_imag[:, None, :] * sine_table[None]
        )
        shifted_imag = (
            stack_imag[:, None, :] * cosines[None] - stack_real[:, None, :] * sine_table[None]
        )
        shifted = (
            jnp.concatenate([shifted_real, shifted_imag], axis=2)
            .astype(jnp.bfloat16)
            .reshape(row_width, FR)
        )
        intersection = lax.dot_general(
            weighted, shifted, (((1,), (1,)), ((), ())), preferred_element_type=jnp.float32
        )
        amplitude = stack_real * stack_real + stack_imag * stack_imag
        ref_power = jnp.dot(
            power_table,
            amplitude.T,
            precision=lax.Precision.HIGHEST,
            preferred_element_type=jnp.float32,
        )
        own_power = jnp.dot(
            group_hot,
            ref_power,
            precision=lax.Precision.HIGHEST,
            preferred_element_type=jnp.float32,
        )
        logits = intersection.reshape(rows_here, R, NS) - 0.5 * own_power[:, :, None]
        return lax.dynamic_update_slice_in_dim(
            table, logits.reshape(rows_here, row_width), offset * row_width, 1
        )

    scores = lax.fori_loop(0, piece.shape[0], add_class, blank)
    slot_prior = jnp.sum(
        jnp.where(
            slot_class[:, None] == jnp.arange(classes, dtype=jnp.int32)[None, :],
            log_prior[None, :],
            0.0,
        ),
        axis=1,
    )
    logits = (
        scores.reshape(rows_here, classes, row_width)
        - 0.5 * data_power[:, None, None]
        + slot_prior[None, :, None]
    )
    row_max = jnp.max(logits, axis=(1, 2), keepdims=True)
    raised = jnp.exp(logits - row_max)
    normaliser = jnp.sum(raised, axis=(1, 2), keepdims=True)
    weights = raised / normaliser
    evidence = row_max[:, 0, 0] + jnp.log(normaliser[:, 0, 0])
    weights_low = weights.astype(jnp.bfloat16)
    group_weights = jnp.dot(
        jnp.sum(weights, axis=2).T,
        group_hot,
        precision=lax.Precision.HIGHEST,
        preferred_element_type=jnp.float32,
    )

    def class_terms(slot_index):
        weight_cols = lax.dynamic_index_in_dim(weights_low, slot_index, 1, keepdims=False)
        moment = lax.dot_general(
            weight_cols, weighted, (((0,), (0,)), ((), ())), preferred_element_type=jnp.float32
        )
        moment = moment.reshape(R, NS, FR)
        moment_real = moment[..., :HALF]
        moment_imag = moment[..., HALF:]
        back_real = jnp.sum(moment_real * cosines[None] - moment_imag * sine_table[None], axis=1)
        back_imag = jnp.sum(moment_imag * cosines[None] + moment_real * sine_table[None], axis=1)
        return jnp.concatenate([back_real, back_imag], axis=1)

    owned = lax.psum_scatter(
        lax.map(
            lambda offset: class_terms(offset),
            jnp.arange(references.shape[0] * lax.axis_size("gx"), dtype=jnp.int32),
        ),
        "gx",
        scatter_dimension=0,
        tiled=True,
    )
    class_sums = lax.psum(owned, "gy")
    totals, evidence_sum = lax.psum((group_weights, jnp.sum(evidence)), ("gx", "gy"))
    own_groups = lax.dynamic_slice_in_dim(totals, lax.axis_index("gx"), 1, 0)
    ctf_power = jnp.dot(
        own_groups,
        ctf_table * ctf_table,
        precision=lax.Precision.HIGHEST,
        preferred_element_type=jnp.float32,
    )
    log_evidence = evidence_sum / (rows_here * lax.axis_size("gx") * lax.axis_size("gy") * HALF)
    return (class_sums, ctf_power, log_evidence)


def solution(mesh):
    return jax.shard_map(
        shards,
        mesh=mesh,
        in_specs=(
            P(("gx", "gy"), None),
            P("gx", None, None),
            P(),
            P(),
            P(),
            P(("gx", "gy")),
            P(),
            P(),
        ),
        out_specs=(P("gx", None, None), P("gx", None), P()),
        check_vma=False,
    )
```

profile of v0, /device:TPU:0, one launch (start us, length us, event | category | flops | bytes accessed | tf_op | source)
XLA Modules:
  0.0 206.5 jit_solution(13460478304987082292)
XLA Ops:
  7.4 2.1 reshape.111
  9.4 1.3 convolution_bitcast_fusion.1
  10.7 0.8 reshape.112
  11.6 4.6 %fusion.46 = f32[64,64,64]{1,2,0:T(8,128)} fusion(f32[64,64,64]{1,0,2:T(8,128)S(1)} %reshape.112), kind=kOutput, calls=%fused_computation.59 | convolution fusion | flops 201383936 | bytes 2097152 | tf_op jit(solution)/shard_map/uy,pyw->puw/dot_general | solution.py:43
  16.2 4.7 %fusion.49 = f32[64,64,64]{1,2,0:T(8,128)} fusion(f32[64,64,64]{1,0,2:T(8,128)S(1)} %reshape.112), kind=kOutput, calls=%fused_computation.60 | convolution fusion | flops 201383936 | bytes 2097152 | tf_op jit(solution)/shard_map/uy,pyw->puw/dot_general | solution.py:46
  21.7 3.4 %multiply_reduce_fusion = (f32[64]{0:T(128)}, f32[64,64,32]{1,2,0:T(8,128)S(1)}, f32[64,64,32]{1,2,0:T(8,128)S(1)}) fusion(f32[64,32]{0,1:T(8,128)S(1)} %copy.44, f32[64,64,64]{1,2,0:T(8,128)} %fusion.49, f32[64,64,64]{1,2,0:T(8,128)} %fusion.46), kind=kLoop, calls=%fused_computation.65 | loop fusion | flops 1179584 | bytes 3154176 | tf_op jit(solution)/shard_map/reduce_sum | solution.py:70
  25.1 1.1 copy.39
  26.1 1.1 copy.40
  27.3 1.1 copy.41
  28.4 1.1 copy.42
  30.3 18.2 %all_gather.3 = bf16[4,12,4096]{2,1,0:T(8,128)(2,1)} all-gather(bf16[1,12,4096]{2,1,0:T(8,128)(2,1)S(1)} %copy-done.3), channel_id=1, replica_groups=mesh['gx'=4,'gy'=8] {'gx'}, dimensions={0}, use_global_device_ids=true | all-gather | bytes 491520 | tf_op jit(solution)/shard_map/all_gather | solution.py:74
  48.4 1.2 multiply_convert_fusion.1
  49.7 25.9 %while.27 = (s32[]{:T(128)}, f32[64,384]{1,0:T(8,128)S(1)}, bf16[4,12,4096]{2,1,0:T(8,128)(2,1)}, bf16[64,4096]{1,0:T(8,128)(2,1)S(1)}, f32[128,2048]{1,0:T(8,12...) while((s32[]{:T(128)}, f32[64,384]{1,0:T(8,128)S(1)}, ...), condition=%wide.region_1.2_spmd.clone.clone, body=%wide.region_0.1_spmd.clone.clone.sunk | while | flops 92814080 | bytes 4696571 | solution.py:112
  49.7 0.9 bitcast_convert_fusion.2
  50.7 1.1 fusion.137
  52.0 0.9 fusion.135
  52.9 0.9 fusion.136
  54.5 1.2 fusion.140
  56.1 0.9 bitcast_convert_fusion.2
  57.1 1.1 fusion.137
  58.4 0.9 fusion.135
  59.3 0.9 fusion.136
  60.9 1.2 fusion.140
  62.7 0.9 bitcast_convert_fusion.2
  63.6 1.1 fusion.137
  64.9 0.9 fusion.135
  65.8 0.9 fusion.136
  67.4 1.2 fusion.140
  69.2 0.9 bitcast_convert_fusion.2
  70.2 1.1 fusion.137
  71.5 0.9 fusion.135
  72.4 0.9 fusion.136
  74.0 1.2 fusion.140
  76.3 0.9 select_reduce_fusion
  78.0 21.0 %while.28 = (s32[]{:T(128)}, f32[4,12,4096]{2,1,0:T(8,128)}, s32[4]{0:T(128)S(1)}, bf16[64,4,96]{0,2,1:T(8,128)(2,1)S(1)}, bf16[64,4096]{1,0:T(8,128)(2,1)S(1)},...) while((s32[]{:T(128)}, f32[4,12,4096]{2,1,0:T(8,128)}, ...), condition=%wide.region_9.10_spmd.clone.clone, body=%wide.region_6.9_spmd.clone.clone.sunk | while | flops 52166660 | bytes 4629223 | solution.py:152
  80.9 1.1 fusion.144
  82.5 0.7 fusion.145
  86.1 1.1 fusion.144
  87.8 0.7 fusion.145
  91.4 1.1 fusion.144
  93.0 0.7 fusion.145
  96.6 1.1 fusion.144
  98.3 0.7 fusion.145
  99.7 0.8 fusion.68
  100.5 42.4 %all-reduce = (f32[4,128]{1,0:T(4,128)S(1)}, f32[]{:T(128)}) all-reduce(f32[4,128]{1,0:T(4,128)S(1)} %fusion.68, f32[]{:T(128)} %add_reduce_fusion.1), channel_id=1, replica_groups=mesh['gx'=4,'gy'=8] {'gx','gy'}, use_global_device_ids=true, to_apply=%region_13.14 | all-reduce | flops 513 | bytes 4104 | tf_op jit(solution)/shard_map/psum | solution.py:161
  143.0 1.2 fusion.54
  144.9 51.8 %all-reduce.3.cloned.1.call-done = f32[1,12,4096]{2,1,0:T(8,128)} async-done(((f32[1,12,4096]{2,1,0:T(8,128)}), f32[1,12,4096]{2,1,0:T(8,128)}) %all-reduce.3.cloned.1.call-update) | async-done | bytes 196624 | tf_op jit(solution)/shard_map/psum | solution.py:160
  196.7 1.8 copy.45
  (69 shorter events, 15.7 us)
Async XLA Ops:
  7.2 135.8 %reduce-scatter.2.cloned.1.call-start = ((), (), s32[]{:S(2)}) async-start(), calls=%async_computation.1 | async-start | bytes 1310720 | tf_op jit(solution)/shard_map/reduce_scatter | solution.py:151
  16.2 5.3 %copy-start.4 = (f32[2048]{0:T(1024)S(1)}, f32[2048]{0:T(1024)}, u32[]{:S(2)}) copy-start(f32[2048]{0:T(1024)} %param.19) | copy-start | bytes 24580
  27.3 2.3 %copy-start = (f32[128,2048]{1,0:T(8,128)S(1)}, f32[128,2048]{1,0:T(8,128)}, u32[]{:S(2)}) copy-start(f32[128,2048]{1,0:T(8,128)} %param.18) | copy-start | bytes 3145732
  28.4 1.3 copy-start.5
  28.4 1.9 copy-start.3
  29.5 18.9 %copy-start.1 = (f32[64,2048]{1,0:T(8,128)S(1)}, f32[64,2048]{1,0:T(8,128)}, u32[]{:S(2)}) copy-start(f32[64,2048]{1,0:T(8,128)} %copy.40) | copy-start | bytes 1572868
  29.5 18.9 %copy-start.2 = (f32[64,2048]{1,0:T(8,128)S(1)}, f32[64,2048]{1,0:T(8,128)}, u32[]{:S(2)}) copy-start(f32[64,2048]{1,0:T(8,128)} %copy.42) | copy-start | bytes 1572868
  99.0 97.7 %all-reduce.3.cloned.1.call-start = ((), (), s32[]{:S(2)}) async-start(), calls=%async_computation.2 | async-start | bytes 524288 | tf_op jit(solution)/shard_map/psum | solution.py:160
Sparse Core Ops, SparseCore 0:
  99.2 29.8 reduce-scatter.1
  143.1 53.5 all-reduce.2
where the time goes:
time: 208 us; the launch traced here: 206 us
  blocking collectives  60.6 us (29%)
  waiting for transfers between devices  51.9 us (25%)
  matrix products  27.2 us (13%)
  other arithmetic  25.1 us (12%)
  local copies, waits for them, and re-layouts  17.6 us (8%)
  between operations  16 us (8%)
  loops' own time  8.13 us (4%)
    psum x1, waiting for transfers between devices, shards(): class_sums = lax.psum(owned, 'gy')  51.8 us
    psum x1, blocking collectives, shards(): lax.psum((group_weights, jnp.sum(evidence)), ('gx', 'gy'))  42.4 us
    all_gather x1, blocking collectives, shards(): piece = lax.all_gather(references, 'gx', axis=0, tiled=True)  18.2 us
    cos x8, other arithmetic, phase_tables(): return (jnp.cos(angles), jnp.sin(angles))  8.53 us
    another operation x1, loops' own time, shards(): lax.map(lambda offset: class_terms(offset), jnp.arange(references.shape[0...  7.85 us
    dot_general x1, matrix products, spectra(): jnp.einsum('uy,pyw->puw', jnp.sin(row_turns), partial_x, precision=lax.Pr...  4.7 us
    dot_general x1, matrix products, spectra(): jnp.einsum('uy,pyw->puw', jnp.cos(row_turns), partial_x, precision=lax.Pr...  4.65 us
    dot_general x4, matrix products, add_class(): lax.dot_general(weighted, shifted, (((1,), (1,)), ((), ())), preferred_el...  4.62 us
  transfers between devices with their start and end apart: 2, of which 1 were waited for; matrix products, arithmetic and copies ran while one was open for 1% of the time, Pallas kernels for 0%

commit v1 on v0

--- a/solution.py
+++ b/solution.py
@@ -9,6 +9,24 @@
 G = 128
 HALF = 2048
 FR = 4096
+
+
+def joined_along(blocks, dim):
+    shape = list(blocks.shape[1:])
+    shape[dim] *= blocks.shape[0]
+    return jnp.moveaxis(blocks, 0, dim).reshape(shape)
+
+
+def doubled(array, axis):
+    size = lax.axis_size(axis)
+    blocks = array[None]
+    for level in range(size.bit_length() - 1):
+        bit = 1 << level
+        theirs = lax.ppermute(blocks, axis, [(i, i ^ bit) for i in range(size)])
+        both = jnp.stack([blocks, theirs])
+        upper = lax.axis_index(axis) >> level & 1
+        blocks = jnp.where(upper == 0, both, both[::-1]).reshape(-1, *array.shape)
+    return blocks
 
 
 def phase_tables(shift_offsets, edge_len):
@@ -71,7 +89,7 @@
     cosines, sine_table = phase_tables(shift_offsets, L)
     power_table = ctf_table * ctf_table * inv_noise
     blank = jnp.zeros((rows_here, classes * row_width), jnp.float32)
-    piece = lax.all_gather(references, "gx", axis=0, tiled=True)
+    piece = joined_along(doubled(references, "gx"), 0)
 
     def add_class(offset, table):
         stack_row = lax.dynamic_index_in_dim(piece, offset, 0, keepdims=False).astype(jnp.float32)

time: 208 us -> 208 us (level)
  blocking collectives: 60.6 us -> 40.5 us
  waiting for transfers between devices: 51.9 us -> 62.9 us
  starting transfers between devices: 0.08 us -> 5.85 us
    all_gather x1 -> x0, blocking collectives: 18.2 us -> none  [shards(): piece = lax.all_gather(references, 'gx', axis=0, tiled=True)]
    ppermute x0 -> x2, waiting for transfers between devices: none -> 11 us  [doubled(): theirs = lax.ppermute(blocks, axis, [(i, i ^ bit) for i in range(size)])]
    ppermute x0 -> x2, starting transfers between devices: none -> 5.77 us  [doubled(): theirs = lax.ppermute(blocks, axis, [(i, i ^ bit) for i in range(size)])]
  transfers between devices with their start and end apart: 2 -> 4, of which waited for: 1 -> 2; matrix products, arithmetic and copies ran while one was open for 1% -> 13% of each run, Pallas kernels for 0% -> 0%
where the time goes in v1:
time: 208 us; the launch traced here: 206 us
  waiting for transfers between devices  62.9 us (30%)
  blocking collectives  40.5 us (19%)
  matrix products  27.3 us (13%)
  other arithmetic  26.7 us (13%)
  local copies, waits for them, and re-layouts  18.7 us (9%)
  between operations  16 us (8%)
  loops' own time  8.12 us (4%)
  starting transfers between devices  5.85 us (3%)
    psum x1, waiting for transfers between devices, shards(): class_sums = lax.psum(owned, 'gy')  51.9 us
    psum x1, blocking collectives, shards(): lax.psum((group_weights, jnp.sum(evidence)), ('gx', 'gy'))  40.5 us
    ppermute x2, waiting for transfers between devices, doubled(): theirs = lax.ppermute(blocks, axis, [(i, i ^ bit) for i in range(size)])  11 us
    cos x8, other arithmetic, phase_tables(): return (jnp.cos(angles), jnp.sin(angles))  8.53 us
    another operation x1, loops' own time, shards(): lax.map(lambda offset: class_terms(offset), jnp.arange(references.shape[0...  7.85 us
    ppermute x2, starting transfers between devices, doubled(): theirs = lax.ppermute(blocks, axis, [(i, i ^ bit) for i in range(size)])  5.77 us
    dot_general x1, matrix products, spectra(): jnp.einsum('uy,pyw->puw', jnp.sin(row_turns), partial_x, precision=lax.Pr...  4.7 us
    dot_general x1, matrix products, spectra(): jnp.einsum('uy,pyw->puw', jnp.cos(row_turns), partial_x, precision=lax.Pr...  4.65 us
  transfers between devices with their start and end apart: 4, of which 2 were waited for; matrix products, arithmetic and copies ran while one was open for 13% of the time, Pallas kernels for 0%

profile of v1, /device:TPU:0, one launch (start us, length us, event | category | flops | bytes accessed | tf_op | source)
XLA Modules:
  0.0 206.2 jit_solution(4508169425790653852)
XLA Ops:
  7.2 3.1 %collective-permute-start = (bf16[1,1,12,4096]{3,2,1,0:T(8,128)(2,1)}, bf16[1,1,12,4096]{3,2,1,0:T(8,128)(2,1)S(1)}, u32[]{:S(2)}, u32[]{:S(2)}) collective-permute-start(bf16[1,1,12,4096]{3,2,1,0:T(8,128)(2,1)} %bitcast.100), channel_id=1, source_target_pairs={{0,8},{8,0},{16,24},{24,16},{1,9},{9,1},{17,25},{25,17},{2,10},{10... | collective-permute-start | bytes 294920 | tf_op jit(solution)/shard_map/ppermute | solution.py:25
  10.5 2.1 reshape.115
  12.6 1.3 convolution_bitcast_fusion.1
  13.8 0.8 reshape.116
  14.7 4.7 %fusion.46 = f32[64,64,64]{1,2,0:T(8,128)} fusion(f32[64,64,64]{1,0,2:T(8,128)S(1)} %reshape.116), kind=kOutput, calls=%fused_computation.59 | convolution fusion | flops 201383936 | bytes 2097152 | tf_op jit(solution)/shard_map/uy,pyw->puw/dot_general | solution.py:61
  19.3 4.7 %fusion.49 = f32[64,64,64]{1,2,0:T(8,128)} fusion(f32[64,64,64]{1,0,2:T(8,128)S(1)} %reshape.116), kind=kOutput, calls=%fused_computation.60 | convolution fusion | flops 201383936 | bytes 2097152 | tf_op jit(solution)/shard_map/uy,pyw->puw/dot_general | solution.py:64
  24.2 2.8 %multiply_reduce_fusion = (f32[64]{0:T(128)S(1)}, f32[64,64,32]{1,2,0:T(8,128)S(1)}, f32[64,64,32]{1,2,0:T(8,128)S(1)}) fusion(f32[64,32]{0,1:T(8,128)S(1)} %copy.44, f32[64,64,64]{1,2,0:T(8,128)} %fusion.49, f32[64,64,64]{1,2,0:T(8,128)} %fusion.46), kind=kLoop, calls=%fused_computation.65 | loop fusion | flops 1179584 | bytes 3154176 | tf_op jit(solution)/shard_map/reduce_sum | solution.py:88
  27.0 1.1 copy.39
  28.1 1.1 copy.40
  29.2 1.1 copy.41
  30.3 1.1 copy.42
  33.7 1.4 multiply_convert_fusion.1
  35.8 2.7 %collective-permute-start.1 = (bf16[2,1,12,4096]{3,2,0,1:T(8,128)(2,1)S(1)}, bf16[2,1,12,4096]{3,2,0,1:T(8,128)(2,1)S(1)}, u32[]{:S(2)}, u32[]{:S(2)}) collective-permute-start(bf16[2,1,12,4096]{3,2,0,1:T(8,128)(2,1)S(1)} %get-tuple-element.382), channel_id=1, source_target_pairs={{0,16},{8,24},{16,0},{24,8},{1,17},{9,25},{17,1},{25,9},{2,18},{10... | collective-permute-start | bytes 589832 | tf_op jit(solution)/shard_map/ppermute | solution.py:25
  39.0 11.0 %collective-permute-done.1 = bf16[2,1,12,4096]{3,2,0,1:T(8,128)(2,1)S(1)} collective-permute-done((bf16[2,1,12,4096]{3,2,0,1:T(8,128)(2,1)S(1)}, bf16[2,1,12,4096]{3,2,0,1:T(8,128)(2,1)S(1)}, u32[]{:S(2)}, u32[]{:S(2)}) %collective-permute-start.1) | collective-permute-done | bytes 196640 | tf_op jit(solution)/shard_map/ppermute | solution.py:25
  50.1 0.9 reverse_select_fusion
  50.9 25.9 %while.27 = (s32[]{:T(128)}, f32[64,384]{1,0:T(8,128)S(1)}, bf16[4,12,4096]{2,1,0:T(8,128)(2,1)}, bf16[64,4096]{1,0:T(8,128)(2,1)S(1)}, f32[128,2048]{1,0:T(8,12...) while((s32[]{:T(128)}, f32[64,384]{1,0:T(8,128)S(1)}, ...), condition=%wide.region_1.2_spmd.clone.clone, body=%wide.region_0.1_spmd.clone.clone.sunk | while | flops 92814080 | bytes 4696571 | solution.py:130
  51.0 0.9 bitcast_convert_fusion.2
  51.9 1.1 fusion.139
  53.2 0.9 fusion.137
  54.1 0.9 fusion.138
  55.7 1.2 fusion.142
  57.4 0.9 bitcast_convert_fusion.2
  58.3 1.1 fusion.139
  59.6 0.9 fusion.137
  60.5 0.9 fusion.138
  62.1 1.2 fusion.142
  63.9 0.9 bitcast_convert_fusion.2
  64.9 1.1 fusion.139
  66.1 0.9 fusion.137
  67.1 0.9 fusion.138
  68.7 1.2 fusion.142
  70.5 0.9 bitcast_convert_fusion.2
  71.4 1.1 fusion.139
  72.7 0.9 fusion.137
  73.6 0.9 fusion.138
  75.2 1.2 fusion.142
  77.0 0.9 fusion.58
  77.9 0.9 exponential_reduce_fusion
  79.6 21.0 %while.28 = (s32[]{:T(128)}, f32[4,12,4096]{2,1,0:T(8,128)}, s32[4]{0:T(128)S(1)}, bf16[64,4,96]{0,2,1:T(8,128)(2,1)S(1)}, bf16[64,4096]{1,0:T(8,128)(2,1)S(1)},...) while((s32[]{:T(128)}, f32[4,12,4096]{2,1,0:T(8,128)}, ...), condition=%wide.region_9.10_spmd.clone.clone, body=%wide.region_6.9_spmd.clone.clone.sunk | while | flops 52166660 | bytes 4629223 | solution.py:170
  82.5 1.1 fusion.146
  87.7 1.1 fusion.146
  93.0 1.1 fusion.146
  98.2 1.1 fusion.146
  101.3 0.8 fusion.70
  102.1 40.5 %all-reduce = (f32[4,128]{1,0:T(4,128)S(1)}, f32[]{:T(128)}) all-reduce(f32[4,128]{1,0:T(4,128)S(1)} %fusion.70, f32[]{:T(128)} %add_reduce_fusion.1), channel_id=1, replica_groups=mesh['gx'=4,'gy'=8] {'gx','gy'}, use_global_device_ids=true, to_apply=%region_13.14 | all-reduce | flops 513 | bytes 4104 | tf_op jit(solution)/shard_map/psum | solution.py:179
  142.6 1.2 fusion.54
  144.5 51.9 %all-reduce.3.cloned.1.call-done = f32[1,12,4096]{2,1,0:T(8,128)} async-done(((f32[1,12,4096]{2,1,0:T(8,128)}), f32[1,12,4096]{2,1,0:T(8,128)}) %all-reduce.3.cloned.1.call-update) | async-done | bytes 196624 | tf_op jit(solution)/shard_map/psum | solution.py:178
  196.4 1.8 copy.45
  (82 shorter events, 20.2 us)
Async XLA Ops:
  7.2 135.4 %reduce-scatter.2.cloned.1.call-start = ((), (), s32[]{:S(2)}) async-start(), calls=%async_computation.1 | async-start | bytes 1310720 | tf_op jit(solution)/shard_map/reduce_scatter | solution.py:169
  7.2 28.5 %collective-permute-start = (bf16[1,1,12,4096]{3,2,1,0:T(8,128)(2,1)}, bf16[1,1,12,4096]{3,2,1,0:T(8,128)(2,1)S(1)}, u32[]{:S(2)}, u32[]{:S(2)}) collective-permute-start(bf16[1,1,12,4096]{3,2,1,0:T(8,128)(2,1)} %bitcast.100), channel_id=1, source_target_pairs={{0,8},{8,0},{16,24},{24,16},{1,9},{9,1},{17,25},{25,17},{2,10},{10... | collective-permute-start | bytes 294920 | tf_op jit(solution)/shard_map/ppermute | solution.py:25
  19.3 4.7 %copy-start.4 = (f32[2048]{0:T(1024)S(1)}, f32[2048]{0:T(1024)}, u32[]{:S(2)}) copy-start(f32[2048]{0:T(1024)} %param.19) | copy-start | bytes 24580
  29.2 2.3 %copy-start = (f32[128,2048]{1,0:T(8,128)S(1)}, f32[128,2048]{1,0:T(8,128)}, u32[]{:S(2)}) copy-start(f32[128,2048]{1,0:T(8,128)} %param.18) | copy-start | bytes 3145732
  30.3 1.3 copy-start.6
  30.3 1.9 copy-start.7
  30.3 1.8 copy-start.8
  30.3 3.3 %copy-start.1 = (f32[64,2048]{1,0:T(8,128)S(1)}, f32[64,2048]{1,0:T(8,128)}, u32[]{:S(2)}) copy-start(f32[64,2048]{1,0:T(8,128)} %copy.40) | copy-start | bytes 1572868
  31.5 2.2 %copy-start.2 = (f32[64,2048]{1,0:T(8,128)S(1)}, f32[64,2048]{1,0:T(8,128)}, u32[]{:S(2)}) copy-start(f32[64,2048]{1,0:T(8,128)} %copy.42) | copy-start | bytes 1572868
  31.6 4.1 %copy-start.3 = (bf16[1,12,4096]{2,1,0:T(8,128)(2,1)S(1)}, bf16[1,12,4096]{2,1,0:T(8,128)(2,1)}, u32[]{:S(2)}) copy-start(bf16[1,12,4096]{2,1,0:T(8,128)(2,1)} %param.13) | copy-start | bytes 294916
  32.3 0.6 copy-start.5
  35.8 14.2 %collective-permute-start.1 = (bf16[2,1,12,4096]{3,2,0,1:T(8,128)(2,1)S(1)}, bf16[2,1,12,4096]{3,2,0,1:T(8,128)(2,1)S(1)}, u32[]{:S(2)}, u32[]{:S(2)}) collective-permute-start(bf16[2,1,12,4096]{3,2,0,1:T(8,128)(2,1)S(1)} %get-tuple-element.382), channel_id=1, source_target_pairs={{0,16},{8,24},{16,0},{24,8},{1,17},{9,25},{17,1},{25,9},{2,18},{10... | collective-permute-start | bytes 589832 | tf_op jit(solution)/shard_map/ppermute | solution.py:25
  100.6 95.8 %all-reduce.3.cloned.1.call-start = ((), (), s32[]{:S(2)}) async-start(), calls=%async_computation.2 | async-start | bytes 524288 | tf_op jit(solution)/shard_map/psum | solution.py:178
Sparse Core Ops, SparseCore 0:
  100.7 28.2 reduce-scatter.1
  142.7 53.6 all-reduce.2
